TPU v7x, 32 devices: a whole 2x2x4 slice. The times are simulated.
32 devices in a mesh: tp: 4 (over y, x), rep: 8 (over z, core).
Axes of the slice: x: 2, y: 2, z: 4, core: 2. Of those that a mesh axis runs over, the one named last changes fastest.
Arguments:
- queries: bfloat16 [128, 4096], P('rep', 'tp'), may hold values from -6 to 6
- new_keys: bfloat16 [128, 2048], P('rep', 'tp'), may hold values from -6 to 6
- new_values: bfloat16 [128, 2048], P('rep', 'tp'), may hold values from -6 to 6
- stored_keys: bfloat16 [128, 16, 128, 128], P('rep', 'tp'), may hold values from -6 to 6
- stored_values: bfloat16 [128, 16, 128, 128], P('rep', 'tp'), may hold values from -6 to 6
- lengths: int32 [128], P('rep'), may hold values from 1 to 128
- out_proj: bfloat16 [4096, 4608], P('tp', 'rep'), may hold values from -0.09375 to 0.09375
- residual: bfloat16 [128, 4608], P(None, 'rep'), may hold values from -4.5 to 4.5
- norm_gain: float32 [4608], replicated, may hold values from 0.1 to 1.9
- embedding: bfloat16 [256000, 4608], P(('tp', 'rep')), may hold values from -1.25 to 1.25
- targets: int32 [128], replicated, may hold values from 0 to 255999
- old_sums: float32 [128], P('rep'), may hold values from -3 to 0
- rewards: float32 [128], P('rep'), may hold values from -6 to 6
- group_ids: int32 [128], P('rep'), may hold values from 0 to 15, as said below
Outputs:
- logprob_sum: float32 [128], P('rep')
- advantage: float32 [128], P('rep')
Inputs may be any that keep to these rules, and one draw needn't show every extreme that they name: `group_ids`: each id names exactly 8 continuations.
All inputs are finite; a program needn't handle non-finite values.
Results may differ from a plain program's by a relative error of at most 0.001.
Values may be sent and summed in bfloat16 or wider, within the bound.
A program may use at most 128 MiB of HBM per device.

v0:
```python
import jax
import jax.numpy as jnp
from jax import lax
from jax.sharding import PartitionSpec as P

GROUP = 8


def attention(queries, new_keys, new_values, stored_keys, stored_values, lengths):
    samp, heads_kv, span, depth = stored_keys.shape
    sample_ratio = queries.shape[1] // (heads_kv * depth)
    query_vector = queries.reshape(samp, heads_kv, sample_ratio, depth)
    scores = (
        jnp.einsum("sgqd,sgpd->sgqp", query_vector, stored_keys, preferred_element_type=jnp.float32)
        / 12.0
    )
    scores = 50.0 * jnp.tanh(scores / 50.0)
    valid = lax.broadcasted_iota(jnp.int32, (samp, 1, 1, span), 3) < lengths[:, None, None, None]
    expo = jnp.where(valid, jnp.exp(scores), 0.0)
    own_logit = (
        jnp.einsum(
            "sgqd,sgd->sgq",
            query_vector,
            new_keys.reshape(samp, heads_kv, depth),
            preferred_element_type=jnp.float32,
        )
        / 12.0
    )
    own_logit = 50.0 * jnp.tanh(own_logit / 50.0)
    own_exp = jnp.exp(own_logit)
    total = jnp.sum(expo, -1) + own_exp
    probs = (expo / total[..., None]).astype(jnp.bfloat16)
    own_probability = (own_exp / total).astype(jnp.bfloat16)
    attended_output = jnp.einsum(
        "sgqp,sgpd->sgqd", probs, stored_values, preferred_element_type=jnp.float32
    )
    attended_output = attended_output + own_probability.astype(jnp.float32)[
        ..., None
    ] * new_values.reshape(samp, heads_kv, 1, depth).astype(jnp.float32)
    return attended_output.reshape(samp, sample_ratio * heads_kv * depth).astype(jnp.bfloat16)


def per_device(
    queries,
    new_keys,
    new_values,
    stored_keys,
    stored_values,
    lengths,
    out_proj,
    residual,
    norm_gain,
    embedding,
    targets,
    old_sums,
    rewards,
    group_ids,
):
    samp = queries.shape[0]
    reps = lax.axis_size("rep")
    rep_index = lax.axis_index("rep")
    tp_index = lax.axis_index("tp")
    groups = samp * reps // GROUP
    member = group_ids[:, None] == lax.broadcasted_iota(jnp.int32, (1, groups), 1)
    reward_part = jnp.sum(jnp.where(member, rewards[:, None], 0.0), 0)
    group_total = lax.psum(reward_part, "rep")
    mine = jnp.sum(jnp.where(member, group_total[None, :], 0.0), 1)
    advantage = rewards - (mine - rewards) / (GROUP - 1.0)
    context = attention(queries, new_keys, new_values, stored_keys, stored_values, lengths)
    partial_value = jnp.dot(
        lax.all_gather(context, "rep", axis=0, tiled=True),
        out_proj,
        preferred_element_type=jnp.float32,
    )
    vocab_rows = embedding.shape[0]
    contract = (((1,), (1,)), ((), ()))
    heads = lax.psum(partial_value, "tp")
    stream = residual.astype(jnp.float32) + heads
    full = lax.all_gather(stream, "rep", axis=1, tiled=True)
    scale = lax.rsqrt(jnp.mean(full * full, axis=1, keepdims=True) + 1e-06)
    normed = (full * scale * norm_gain[None, :]).astype(jnp.bfloat16)
    logits = lax.dot_general(normed, embedding, contract, preferred_element_type=jnp.float32)
    capped = 30.0 * jnp.tanh(logits / 30.0)
    offset = (tp_index * reps + rep_index) * vocab_rows
    entry_ids = offset + lax.broadcasted_iota(jnp.int32, (1, vocab_rows), 1)
    picked_part = jnp.sum(jnp.where(entry_ids == targets[:, None], capped, 0.0), 1)
    total, picked = lax.psum((jnp.sum(jnp.exp(capped), 1), picked_part), ("tp", "rep"))
    logprob = picked - jnp.log(total)
    own_rows = lax.dynamic_slice_in_dim(logprob, rep_index * samp, samp)
    logprob_sum = old_sums + own_rows
    return (logprob_sum, advantage)


def solution(mesh):
    in_specs = (
        P("rep", "tp"),
        P("rep", "tp"),
        P("rep", "tp"),
        P("rep", "tp", None, None),
        P("rep", "tp", None, None),
        P("rep"),
        P("tp", "rep"),
        P(None, "rep"),
        P(),
        P(("tp", "rep"), None),
        P(),
        P("rep"),
        P("rep"),
        P("rep"),
    )
    out_specs = (P("rep"), P("rep"))
    return jax.shard_map(
        per_device, mesh=mesh, in_specs=in_specs, out_specs=out_specs, check_vma=False
    )
```

profile of v0, /device:TPU:0, one launch (start us, length us, event | category | flops | bytes accessed | tf_op | source)
XLA Modules:
  0.0 191.0 jit_solution(11185303319291343823)
XLA Ops:
  7.2 0.0 copy-start
  7.2 0.0 copy-start.4
  7.2 0.0 all-reduce.3.cloned.1.call-start
  7.2 0.9 reshape.60
  8.2 0.7 iota_compare_fusion.1
  8.9 0.0 copy-done
  8.9 1.3 fusion.15
  10.2 0.0 copy-start.2
  10.2 0.1 copy.18
  10.3 0.8 reshape.66
  11.1 0.2 fusion.16
  11.3 0.1 copy.22
  11.4 0.1 copy.19
  11.6 0.1 copy.20
  11.7 0.0 copy-done.4
  11.7 0.6 reshape.62
  12.3 0.0 copy-start.3
  12.3 2.9 %fusion.8 = bf16[16,4,2,128]{3,2,1,0:T(2,128)(2,1)} fusion(bf16[16,4,128,128]{3,2,1,0:T(8,128)(2,1)} %param.18, f32[16,4,2,128]{3,2,1,0:T(2,128)S(1)} %get-tuple-element.9, f32[16,4,128]{2,1,0:T(4,128)} %reshape.62, f32[16,4,2]{2,1,0:T(4,128)S(1)} %copy.20, f32[16,4,2]{2,1,0:T(4,128)S(1)} %copy.19), kind=kOutput, calls=%fused_computation.15 | convolution fusion | flops 4276224 | bytes 2229248 | tf_op jit(solution)/shard_map/sgqp,sgpd->sgqd/dot_general | solution.py:34
  15.2 0.0 copy-start.7
  15.2 0.0 copy-start.8
  15.2 0.8 convert_element_type.39
  16.1 15.9 %all_gather.6 = bf16[128,1024]{1,0:T(8,128)(2,1)S(1)} all-gather(bf16[16,1024]{1,0:T(8,128)(2,1)S(1)} %convert_element_type.39), channel_id=1, replica_groups=mesh['tp'=4,'rep'=8] {'rep'}, dimensions={0}, use_global_device_ids=true | all-gather | bytes 294912 | tf_op jit(solution)/shard_map/all_gather | solution.py:71
  32.0 0.0 copy-done.2
  32.0 0.0 copy-start.6
  32.0 0.0 copy-start.9
  32.0 1.2 fusion.17
  33.2 0.0 all-reduce.3.cloned.1.call-update
  33.2 0.0 all-gather.2.cloned.1.call-start
  33.2 44.5 %all-reduce.3.cloned.1.call-done = f32[128,576]{0,1:T(8,128)} async-done(((f32[128,576]{0,1:T(8,128)}), f32[128,576]{0,1:T(8,128)}) %all-reduce.3.cloned.1.call-update) | async-done | bytes 294928 | tf_op jit(solution)/shard_map/psum | solution.py:77
  77.7 0.0 copy-done.3
  77.7 1.7 convert_add_fusion
  79.4 0.0 all-gather.2.cloned.1.call-update
  79.5 0.0 copy-done.7
  79.5 0.0 copy-done.8
  79.5 0.1 select_reduce_fusion.2
  79.6 16.4 %psum.31 = f32[16]{0:T(128)S(1)} all-reduce(f32[16]{0:T(128)S(1)} %select_reduce_fusion.2), channel_id=1, replica_groups=mesh['tp'=4,'rep'=8] {'rep'}, use_global_device_ids=true, to_apply=%region_8.9 | all-reduce | flops 16 | bytes 128 | tf_op jit(solution)/shard_map/psum | solution.py:66
  96.0 0.2 select_reduce_fusion.1
  96.2 0.5 multiply_subtract_fusion
  96.7 14.5 %all-gather.2.cloned.1.call-done = f32[128,4608]{0,1:T(8,128)} async-done(((f32[128,576]{0,1:T(8,128)}), f32[128,4608]{0,1:T(8,128)}) %all-gather.2.cloned.1.call-update) | async-done | bytes 2359312 | tf_op jit(solution)/shard_map/all_gather | solution.py:79
  111.2 0.0 copy-start.1
  111.2 2.4 %multiply_reduce_fusion = f32[128]{0:T(128)S(1)} fusion(f32[128,4608]{0,1:T(8,128)} %all-gather.2.cloned.1.call-done), kind=kLoop, calls=%fused_computation.6 | loop fusion | flops 1179520 | bytes 2359808 | tf_op jit(solution)/shard_map/reduce_sum | solution.py:80
  113.6 0.0 copy-done.6
  113.6 0.0 copy-done.9
  113.6 0.0 copy-done.1
  113.7 0.0 copy-start.5
  113.7 30.2 %exponential_reduce_fusion = (f32[128]{0:T(128)S(1)}, f32[128]{0:T(128)S(1)}) fusion(s32[128]{0:T(128)S(1)} %copy-done.9, s32[8000]{0:T(1024)S(1)} %iota_add_fusion, bf16[8000,4608]{1,0:T(8,128)(2,1)} %param.23, f32[128,4608]{0,1:T(8,128)S(1)} %copy-done.1, f32[4608]{0:T(1024)S(1)} %copy-done.6, f32[128]{0:T(128)S(1)} %add_rsqrt_fusion), kind=kOutput, calls=%fused_computation.3 | convolution fusion | flops 9445097472 | bytes 76139776 | tf_op jit(solution)/shard_map/dot_general | solution.py:82
  143.8 39.7 %all-reduce = (f32[128]{0:T(128)S(1)}, f32[128]{0:T(128)S(1)}) all-reduce(f32[128]{0:T(128)S(1)} %get-tuple-element.3, f32[128]{0:T(128)S(1)} %get-tuple-element.2), channel_id=1, replica_groups=mesh['tp'=4,'rep'=8] {'tp','rep'}, use_global_device_ids=true, to_apply=%region_4.5 | all-reduce | flops 256 | bytes 2048 | tf_op jit(solution)/shard_map/psum | solution.py:87
  183.6 0.0 copy-done.5
  183.6 0.6 dynamic-slice_add_fusion
  (4 shorter events, 0.0 us)
Async XLA Ops:
  7.2 1.7 copy-start
  7.2 4.5 %copy-start.4 = (bf16[16,512]{1,0:T(8,128)(2,1)S(1)}, bf16[16,512]{1,0:T(8,128)(2,1)}, u32[]{:S(2)}) copy-start(bf16[16,512]{1,0:T(8,128)(2,1)} %param.16) | copy-start | bytes 49156
  7.2 70.5 %all-reduce.3.cloned.1.call-start = ((), (), s32[]{:S(2)}) async-start(), calls=%async_computation | async-start | bytes 589824 | tf_op jit(solution)/shard_map/psum | solution.py:77
  10.2 21.8 %copy-start.2 = (bf16[1024,576]{0,1:T(8,128)(2,1)S(1)}, bf16[1024,576]{0,1:T(8,128)(2,1)}, u32[]{:S(2)}) copy-start(bf16[1024,576]{0,1:T(8,128)(2,1)} %param.20) | copy-start | bytes 3538948
  12.3 65.4 %copy-start.3 = (bf16[128,576]{0,1:T(8,128)(2,1)S(1)}, bf16[128,576]{0,1:T(8,128)(2,1)}, u32[]{:S(2)}) copy-start(bf16[128,576]{0,1:T(8,128)(2,1)} %param.21) | copy-start | bytes 442372
  15.2 64.2 %copy-start.7 = (s32[16]{0:T(128)S(1)}, s32[16]{0:T(128)}, u32[]{:S(2)}) copy-start(s32[16]{0:T(128)} %param.27) | copy-start | bytes 196
  15.2 64.2 %copy-start.8 = (f32[16]{0:T(128)S(1)}, f32[16]{0:T(128)}, u32[]{:S(2)}) copy-start(f32[16]{0:T(128)} %param.26) | copy-start | bytes 196
  32.0 81.7 %copy-start.6 = (f32[4608]{0:T(1024)S(1)}, f32[4608]{0:T(1024)}, u32[]{:S(2)}) copy-start(f32[4608]{0:T(1024)} %param.22) | copy-start | bytes 55300
  32.0 81.7 %copy-start.9 = (s32[128]{0:T(128)S(1)}, s32[128]{0:T(128)}, u32[]{:S(2)}) copy-start(s32[128]{0:T(128)} %param.24) | copy-start | bytes 1540
  33.2 78.0 %all-gather.2.cloned.1.call-start = ((), (), s32[]{:S(2)}) async-start(), calls=%async_computation.1 | async-start | bytes 2654208 | tf_op jit(solution)/shard_map/all_gather | solution.py:79
  111.2 2.5 %copy-start.1 = (f32[128,4608]{0,1:T(8,128)S(1)}, f32[128,4608]{0,1:T(8,128)}, u32[]{:S(2)}) copy-start(f32[128,4608]{0,1:T(8,128)} %all-gather.2.cloned.1.call-done) | copy-start | bytes 7077892
  113.7 69.9 %copy-start.5 = (f32[16]{0:T(128)S(1)}, f32[16]{0:T(128)}, u32[]{:S(2)}) copy-start(f32[16]{0:T(128)} %param.25) | copy-start | bytes 196
Sparse Core Ops, SparseCore 0:
  33.3 44.3 all-reduce.2
  79.6 31.5 all-gather.1
where the time goes:
time: 191 us
  blocking collectives  72.1 us (38%)
  waiting for transfers between devices  59 us (31%)
  matrix products  35.8 us (19%)
  between operations  14.1 us (7%)
  other arithmetic  6.3 us (3%)
  local copies, waits for them, and re-layouts  3.63 us (2%)
    psum x1, waiting for transfers between devices, per_device(): heads = lax.psum(partial_value, 'tp')  44.5 us
    psum x1, blocking collectives, per_device(): lax.psum((jnp.sum(jnp.exp(capped), 1), picked_part), ('tp', 'rep'))  39.7 us
    dot_general x1, matrix products, per_device(): lax.dot_general(normed, embedding, contract, preferred_element_type=jnp.f...  30.2 us
    psum x1, blocking collectives, per_device(): group_total = lax.psum(reward_part, 'rep')  16.4 us
    all_gather x1, blocking collectives, per_device(): lax.all_gather(context, 'rep', axis=0, tiled=True)  15.9 us
    all_gather x1, waiting for transfers between devices, per_device(): full = lax.all_gather(stream, 'rep', axis=1, tiled=True)  14.5 us
  transfers between devices with their start and end apart: 2, of which 2 were waited for; matrix products, arithmetic and copies ran while one was open for 0% of the time, Pallas kernels for 0%

commit v1 on v0

--- a/solution.py
+++ b/solution.py
@@ -84,7 +84,7 @@
     offset = (tp_index * reps + rep_index) * vocab_rows
     entry_ids = offset + lax.broadcasted_iota(jnp.int32, (1, vocab_rows), 1)
     picked_part = jnp.sum(jnp.where(entry_ids == targets[:, None], capped, 0.0), 1)
-    total, picked = lax.psum((jnp.sum(jnp.exp(capped), 1), picked_part), ("tp", "rep"))
+    total, picked = lax.psum(lax.psum((jnp.sum(jnp.exp(capped), 1), picked_part), "rep"), "tp")
     logprob = picked - jnp.log(total)
     own_rows = lax.dynamic_slice_in_dim(logprob, rep_index * samp, samp)
     logprob_sum = old_sums + own_rows

time: 191 us -> 177 us (0.927)
  blocking collectives: 72.1 us -> 40.8 us
  waiting for transfers between devices: 59 us -> 76 us
    psum x2, blocking collectives: 56.1 us -> 24.9 us  [the longest x1 15.1 us: per_device(): lax.psum((jnp.sum(jnp.exp(capped), 1), picked_part), 'rep')]
    all_gather x1, waiting for transfers between devices: 14.5 us -> 31.5 us  [per_device(): full = lax.all_gather(stream, 'rep', axis=1, tiled=True)]
where the time goes in v1:
time: 177 us
  waiting for transfers between devices  76 us (43%)
  blocking collectives  40.8 us (23%)
  matrix products  35.8 us (20%)
  between operations  14.1 us (8%)
  other arithmetic  6.3 us (4%)
  local copies, waits for them, and re-layouts  3.63 us (2%)
    psum x1, waiting for transfers between devices, per_device(): heads = lax.psum(partial_value, 'tp')  44.5 us
    all_gather x1, waiting for transfers between devices, per_device(): full = lax.all_gather(stream, 'rep', axis=1, tiled=True)  31.5 us
    dot_general x1, matrix products, per_device(): lax.dot_general(normed, embedding, contract, preferred_element_type=jnp.f...  30.2 us
    all_gather x1, blocking collectives, per_device(): lax.all_gather(context, 'rep', axis=0, tiled=True)  15.9 us
    psum x1, blocking collectives, per_device(): lax.psum((jnp.sum(jnp.exp(capped), 1), picked_part), 'rep')  15.1 us
    psum x1, blocking collectives, per_device(): lax.psum(lax.psum((jnp.sum(jnp.exp(capped), 1), picked_part), 'rep'), 'tp')  9.81 us
  transfers between devices with their start and end apart: 2, of which 2 were waited for; matrix products, arithmetic and copies ran while one was open for 0% of the time, Pallas kernels for 0%

profile of v1, /device:TPU:0, one launch (start us, length us, event | category | flops | bytes accessed | tf_op | source)
XLA Modules:
  0.0 176.7 jit_solution(15862483424096703027)
XLA Ops:
  7.2 0.0 copy-start
  7.2 0.0 copy-start.4
  7.2 0.0 all-reduce.4.cloned.1.call-start
  7.2 0.9 reshape.60
  8.2 0.7 iota_compare_fusion.1
  8.9 0.0 copy-done
  8.9 1.3 fusion.15
  10.2 0.0 copy-start.2
  10.2 0.1 copy.18
  10.3 0.8 reshape.66
  11.1 0.2 fusion.16
  11.3 0.1 copy.22
  11.4 0.1 copy.19
  11.6 0.1 copy.20
  11.7 0.0 copy-done.4
  11.7 0.6 reshape.62
  12.3 0.0 copy-start.3
  12.3 2.9 %fusion.8 = bf16[16,4,2,128]{3,2,1,0:T(2,128)(2,1)} fusion(bf16[16,4,128,128]{3,2,1,0:T(8,128)(2,1)} %param.18, f32[16,4,2,128]{3,2,1,0:T(2,128)S(1)} %get-tuple-element.12, f32[16,4,128]{2,1,0:T(4,128)} %reshape.62, f32[16,4,2]{2,1,0:T(4,128)S(1)} %copy.20, f32[16,4,2]{2,1,0:T(4,128)S(1)} %copy.19), kind=kOutput, calls=%fused_computation.15 | convolution fusion | flops 4276224 | bytes 2229248 | tf_op jit(solution)/shard_map/sgqp,sgpd->sgqd/dot_general | solution.py:34
  15.2 0.0 copy-start.8
  15.2 0.0 copy-start.9
  15.2 0.8 convert_element_type.39
  16.1 15.9 %all_gather.6 = bf16[128,1024]{1,0:T(8,128)(2,1)S(1)} all-gather(bf16[16,1024]{1,0:T(8,128)(2,1)S(1)} %convert_element_type.39), channel_id=1, replica_groups=mesh['tp'=4,'rep'=8] {'rep'}, dimensions={0}, use_global_device_ids=true | all-gather | bytes 294912 | tf_op jit(solution)/shard_map/all_gather | solution.py:71
  32.0 0.0 copy-done.2
  32.0 0.0 copy-start.6
  32.0 0.0 copy-start.7
  32.0 1.2 fusion.17
  33.2 0.0 all-reduce.4.cloned.1.call-update
  33.2 0.0 all-gather.2.cloned.1.call-start
  33.2 44.5 %all-reduce.4.cloned.1.call-done = f32[128,576]{0,1:T(8,128)} async-done(((f32[128,576]{0,1:T(8,128)}), f32[128,576]{0,1:T(8,128)}) %all-reduce.4.cloned.1.call-update) | async-done | bytes 294928 | tf_op jit(solution)/shard_map/psum | solution.py:77
  77.7 0.0 copy-done.3
  77.7 1.7 convert_add_fusion
  79.4 0.0 all-gather.2.cloned.1.call-update
  79.5 0.0 copy-done.8
  79.5 0.0 copy-done.9
  79.5 0.1 select_reduce_fusion.2
  79.6 31.5 %all-gather.2.cloned.1.call-done = f32[128,4608]{0,1:T(8,128)} async-done(((f32[128,576]{0,1:T(8,128)}), f32[128,4608]{0,1:T(8,128)}) %all-gather.2.cloned.1.call-update) | async-done | bytes 2359312 | tf_op jit(solution)/shard_map/all_gather | solution.py:79
  111.1 0.0 copy-start.1
  111.1 2.4 %multiply_reduce_fusion = f32[128]{0:T(128)S(1)} fusion(f32[128,4608]{0,1:T(8,128)} %all-gather.2.cloned.1.call-done), kind=kLoop, calls=%fused_computation.6 | loop fusion | flops 1179520 | bytes 2359808 | tf_op jit(solution)/shard_map/reduce_sum | solution.py:80
  113.5 0.0 copy-done.6
  113.5 0.0 copy-done.7
  113.5 0.0 copy-done.1
  113.5 0.0 copy-start.5
  113.5 30.2 %exponential_reduce_fusion = (f32[128]{0:T(128)S(1)}, f32[128]{0:T(128)S(1)}) fusion(s32[128]{0:T(128)S(1)} %copy-done.7, s32[8000]{0:T(1024)S(1)} %iota_add_fusion, bf16[8000,4608]{1,0:T(8,128)(2,1)} %param.23, f32[128,4608]{0,1:T(8,128)S(1)} %copy-done.1, f32[4608]{0:T(1024)S(1)} %copy-done.6, f32[128]{0:T(128)S(1)} %add_rsqrt_fusion), kind=kOutput, calls=%fused_computation.3 | convolution fusion | flops 9445097472 | bytes 76139776 | tf_op jit(solution)/shard_map/dot_general | solution.py:82
  143.7 15.1 %all-reduce = (f32[128]{0:T(128)S(1)}, f32[128]{0:T(128)S(1)}, f32[16]{0:T(128)S(1)}) all-reduce(f32[128]{0:T(128)S(1)} %get-tuple-element.3, f32[128]{0:T(128)S(1)} %get-tuple-element.2, f32[16]{0:T(128)S(1)} %select_reduce_fusion.2), channel_id=1, replica_groups=mesh['tp'=4,'rep'=8] {'rep'}, use_global_device_ids=true, to_apply=%region_4.5 | all-reduce | flops 272 | bytes 2176 | tf_op jit(solution)/shard_map/psum | solution.py:87
  158.8 0.2 select_reduce_fusion.1
  159.0 0.5 multiply_subtract_fusion
  159.5 9.8 %all-reduce.1 = (f32[128]{0:T(128)S(1)}, f32[128]{0:T(128)S(1)}) all-reduce(f32[128]{0:T(128)S(1)} %get-tuple-element.4, f32[128]{0:T(128)S(1)} %get-tuple-element.5), channel_id=1, replica_groups=mesh['tp'=4,'rep'=8] {'tp'}, use_global_device_ids=true, to_apply=%region_5.6 | all-reduce | flops 256 | bytes 2048 | tf_op jit(solution)/shard_map/psum | solution.py:87
  169.3 0.0 copy-done.5
  169.3 0.6 dynamic-slice_add_fusion
  (4 shorter events, 0.1 us)
Async XLA Ops:
  7.2 1.7 copy-start
  7.2 4.5 %copy-start.4 = (bf16[16,512]{1,0:T(8,128)(2,1)S(1)}, bf16[16,512]{1,0:T(8,128)(2,1)}, u32[]{:S(2)}) copy-start(bf16[16,512]{1,0:T(8,128)(2,1)} %param.16) | copy-start | bytes 49156
  7.2 70.5 %all-reduce.4.cloned.1.call-start = ((), (), s32[]{:S(2)}) async-start(), calls=%async_computation | async-start | bytes 589824 | tf_op jit(solution)/shard_map/psum | solution.py:77
  10.2 21.8 %copy-start.2 = (bf16[1024,576]{0,1:T(8,128)(2,1)S(1)}, bf16[1024,576]{0,1:T(8,128)(2,1)}, u32[]{:S(2)}) copy-start(bf16[1024,576]{0,1:T(8,128)(2,1)} %param.20) | copy-start | bytes 3538948
  12.3 65.4 %copy-start.3 = (bf16[128,576]{0,1:T(8,128)(2,1)S(1)}, bf16[128,576]{0,1:T(8,128)(2,1)}, u32[]{:S(2)}) copy-start(bf16[128,576]{0,1:T(8,128)(2,1)} %param.21) | copy-start | bytes 442372
  15.2 64.2 %copy-start.8 = (s32[16]{0:T(128)S(1)}, s32[16]{0:T(128)}, u32[]{:S(2)}) copy-start(s32[16]{0:T(128)} %param.27) | copy-start | bytes 196
  15.2 64.2 %copy-start.9 = (f32[16]{0:T(128)S(1)}, f32[16]{0:T(128)}, u32[]{:S(2)}) copy-start(f32[16]{0:T(128)} %param.26) | copy-start | bytes 196
  32.0 81.5 %copy-start.6 = (f32[4608]{0:T(1024)S(1)}, f32[4608]{0:T(1024)}, u32[]{:S(2)}) copy-start(f32[4608]{0:T(1024)} %param.22) | copy-start | bytes 55300
  32.0 81.5 %copy-start.7 = (s32[128]{0:T(128)S(1)}, s32[128]{0:T(128)}, u32[]{:S(2)}) copy-start(s32[128]{0:T(128)} %param.24) | copy-start | bytes 1540
  33.2 77.9 %all-gather.2.cloned.1.call-start = ((), (), s32[]{:S(2)}) async-start(), calls=%async_computation.1 | async-start | bytes 2654208 | tf_op jit(solution)/shard_map/all_gather | solution.py:79
  111.1 2.5 %copy-start.1 = (f32[128,4608]{0,1:T(8,128)S(1)}, f32[128,4608]{0,1:T(8,128)}, u32[]{:S(2)}) copy-start(f32[128,4608]{0,1:T(8,128)} %all-gather.2.cloned.1.call-done) | copy-start | bytes 7077892
  113.5 55.8 %copy-start.5 = (f32[16]{0:T(128)S(1)}, f32[16]{0:T(128)}, u32[]{:S(2)}) copy-start(f32[16]{0:T(128)} %param.25) | copy-start | bytes 196
Sparse Core Ops, SparseCore 0:
  33.3 44.3 all-reduce.3
  79.6 31.4 all-gather.1
